TPU v7x, 512 devices: a whole 4x4x16 slice. The times are simulated.
512 devices in a mesh: row: 32 (over x, z_lo, core), col: 16 (over y, z_hi).
Axes of the slice: x: 4, y: 4, z: 16 (z_hi: 4, z_lo: 4; z = z_hi * 4 + z_lo), core: 2. Of those that a mesh axis runs over, the one named last changes fastest.
Arguments:
- features: bfloat16 [65536, 128], P(('row', 'col')), may hold values from -6 to 6
- weight: bfloat16 [128, 128], replicated, may hold values from -0.5 to 0.5
- adj_values: bfloat16 [32, 16, 16, 128, 128], P('row', 'col'), may hold values from -0.125 to 0.125
- tile_rows: int32 [32, 16, 16], P('row', 'col'), may hold values from 0 to 15
- tile_cols: int32 [32, 16, 16], P('row', 'col'), may hold values from 0 to 31
- cotangent: bfloat16 [65536, 128], P(('row', 'col')), may hold values from -6 to 6
Outputs:
- activations: float32 [65536, 128], P(('row', 'col'))
- grad_features: float32 [65536, 128], P(('row', 'col'))
- grad_weight: float32 [128, 128], replicated
All inputs are finite; a program needn't handle non-finite values.
Results may differ from a plain program's by a relative error of at most 0.0049.
Values may be sent and summed in bfloat16 or wider, within the bound.
No kernel may reach another device: no remote copies, remote signals or barrier semaphores. Data moves between devices by JAX's collectives and lax.ppermute only.
A program may use at most 64 MiB of HBM per device.

v0:
```python
import jax
import jax.numpy as jnp
from jax import lax
from jax.sharding import PartitionSpec as P


def per_device(features, weight, adj_values, tile_rows, tile_cols, cotangent):
    blocks = adj_values[0, 0]
    rows_id = tile_rows[0, 0]
    cols_id = tile_cols[0, 0]
    tile = blocks.shape[-1]
    owned = features.shape[0]
    width = features.shape[1]
    n_row = lax.axis_size("row")
    n_col = lax.axis_size("col")
    col_block = lax.all_gather(features, "row", axis=0, tiled=True)
    picked = col_block.reshape(-1, tile, width)[cols_id]
    prods = jnp.einsum("tab,tbf->taf", blocks, picked, preferred_element_type=jnp.float32)
    partial_rows = jax.ops.segment_sum(prods, rows_id, num_segments=n_col * owned // tile)
    aggregated = lax.psum_scatter(
        partial_rows.reshape(-1, width), "col", scatter_dimension=0, tiled=True
    )
    zed = aggregated.astype(jnp.bfloat16)
    pre = jnp.dot(zed, weight, preferred_element_type=jnp.float32)
    sig = jax.nn.sigmoid(pre)
    activations = pre * sig
    dpre = (cotangent.astype(jnp.float32) * sig * (1.0 + pre * (1.0 - sig))).astype(jnp.bfloat16)
    weight_part = lax.dot_general(
        zed, dpre, (((0,), (0,)), ((), ())), preferred_element_type=jnp.float32
    )
    grad_weight = lax.psum(weight_part, ("row", "col"))
    dzed = lax.dot_general(
        dpre, weight, (((1,), (1,)), ((), ())), preferred_element_type=jnp.float32
    ).astype(jnp.bfloat16)
    row_block = lax.all_gather(dzed, "col", axis=0, tiled=True)
    picked_back = row_block.reshape(-1, tile, width)[rows_id]
    prods_back = jnp.einsum("tab,taf->tbf", blocks, picked_back, preferred_element_type=jnp.float32)
    partial_cols = jax.ops.segment_sum(prods_back, cols_id, num_segments=n_row * owned // tile)
    grad_features = lax.psum_scatter(
        partial_cols.reshape(-1, width), "row", scatter_dimension=0, tiled=True
    )
    return (activations, grad_features, grad_weight)


def solution(mesh):
    return jax.shard_map(
        per_device,
        mesh=mesh,
        in_specs=(
            P(("row", "col"), None),
            P(),
            P("row", "col", None, None, None),
            P("row", "col", None),
            P("row", "col", None),
            P(("row", "col"), None),
        ),
        out_specs=(P(("row", "col"), None), P(("row", "col"), None), P()),
        check_vma=False,
    )
```

profile of v0, /device:TPU:16, one launch (start us, length us, event | category | flops | bytes accessed | tf_op | source)
XLA Modules:
  0.0 806.1 jit_solution(2386239688956795602)
XLA Ops:
  7.2 0.0 copy-start
  7.2 0.0 all-gather.2.cloned.1.call-start
  7.2 0.7 all-gather.2.cloned.1.call-update
  7.9 0.0 reduce-scatter.3.cloned.1.call-start
  8.0 0.7 fusion.7
  8.6 69.6 %all-gather.2.cloned.1.call-done = bf16[4096,128]{1,0:T(8,128)(2,1)} async-done(((bf16[128,128]{1,0:T(8,128)(2,1)}), bf16[4096,128]{1,0:T(8,128)(2,1)}) %all-gather.2.cloned.1.call-update) | async-done | bytes 1048592 | tf_op jit(solution)/shard_map/all_gather | solution.py:16
  78.3 1.9 gather_fusion
  80.2 0.5 convolution_bitcast_fusion.1
  80.7 0.3 copy.12
  81.0 0.1 broadcast_in_dim.8
  81.1 0.2 copy-done.4
  81.3 1.6 scatter_fusion
  83.0 1.0 copy-done.2
  83.9 0.0 reduce-scatter.3.cloned.1.call-update
  83.9 0.0 all-reduce.2.cloned.1.call-start
  84.0 112.7 %reduce-scatter.3.cloned.1.call-done = f32[128,128]{1,0:T(8,128)} async-done(((f32[2048,128]{1,0:T(8,128)}), f32[128,128]{1,0:T(8,128)}) %reduce-scatter.3.cloned.1.call-update) | async-done | bytes 65552 | tf_op jit(solution)/shard_map/reduce_scatter | solution.py:20
  196.7 1.6 multiply_convert_fusion
  198.3 0.1 convolution_convert_fusion
  198.4 1.7 fusion.3
  200.1 0.0 all-reduce.2.cloned.1.call-update
  200.2 0.0 reduce-scatter.5.cloned.1.call-start
  200.2 52.1 %all_gather.7 = bf16[2048,128]{1,0:T(8,128)(2,1)S(1)} all-gather(bf16[128,128]{1,0:T(8,128)(2,1)S(1)} %convolution_convert_fusion), channel_id=1, replica_groups=mesh['row'=32,'col'=16] {'col'}, dimensions={0}, use_global_device_ids=true | all-gather | bytes 557056 | tf_op jit(solution)/shard_map/all_gather | solution.py:35
  252.3 0.6 gather_fusion.1
  252.9 0.4 convolution_bitcast_fusion
  253.3 1.3 copy.14
  254.6 0.2 broadcast_in_dim.9
  254.8 2.6 scatter_fusion.1
  257.5 1.3 copy-done.1
  258.8 0.0 reduce-scatter.5.cloned.1.call-update
  258.8 389.8 %all-reduce.2.cloned.1.call-done = f32[128,128]{1,0:T(8,128)} async-done(((f32[128,128]{1,0:T(8,128)}), f32[128,128]{1,0:T(8,128)}) %all-reduce.2.cloned.1.call-update) | async-done | bytes 65552 | tf_op jit(solution)/shard_map/psum | solution.py:31
  648.6 149.5 %reduce-scatter.5.cloned.1.call-done = f32[128,128]{1,0:T(8,128)} async-done(((f32[4096,128]{1,0:T(8,128)}), f32[128,128]{1,0:T(8,128)}) %reduce-scatter.5.cloned.1.call-update) | async-done | bytes 65552 | tf_op jit(solution)/shard_map/reduce_scatter | solution.py:39
  798.1 1.5 copy.20
  (13 shorter events, 0.0 us)
Async XLA Ops:
  7.2 73.0 %copy-start = (bf16[1,1,16,128,128]{4,3,2,1,0:T(8,128)(2,1)S(1)}, bf16[1,1,16,128,128]{4,3,2,1,0:T(8,128)(2,1)}, u32[]{:S(2)}) copy-start(bf16[1,1,16,128,128]{4,3,2,1,0:T(8,128)(2,1)} %param.8) | copy-start | bytes 1572868
  7.2 71.1 %all-gather.2.cloned.1.call-start = ((), (), s32[]{:S(2)}) async-start(), calls=%async_computation.2 | async-start | bytes 1081344 | tf_op jit(solution)/shard_map/all_gather | solution.py:16
  7.9 188.8 %reduce-scatter.3.cloned.1.call-start = ((), (), s32[]{:S(2)}) async-start(), calls=%async_computation.3 | async-start | bytes 1114112 | tf_op jit(solution)/shard_map/reduce_scatter | solution.py:20
  80.7 0.7 copy-start.4
  81.3 115.3 %copy-start.3 = (bf16[128,128]{1,0:T(8,128)(2,1)S(1)}, bf16[128,128]{1,0:T(8,128)(2,1)}, u32[]{:S(2)}) copy-start(bf16[128,128]{1,0:T(8,128)(2,1)} %param.7) | copy-start | bytes 98308
  81.3 115.3 %copy-start.6 = (bf16[128,128]{1,0:T(8,128)(2,1)S(1)}, bf16[128,128]{1,0:T(8,128)(2,1)}, u32[]{:S(2)}) copy-start(bf16[128,128]{1,0:T(8,128)(2,1)} %param.11) | copy-start | bytes 98308
  82.9 1.0 copy-start.2
  83.9 564.6 %all-reduce.2.cloned.1.call-start = ((), (), s32[]{:S(2)}) async-start(), calls=%async_computation.5 | async-start | bytes 131072 | tf_op jit(solution)/shard_map/psum | solution.py:31
  200.2 597.9 %reduce-scatter.5.cloned.1.call-start = ((), (), s32[]{:S(2)}) async-start(), calls=%async_computation.4 | async-start | bytes 2162688 | tf_op jit(solution)/shard_map/reduce_scatter | solution.py:39
  253.3 1.6 copy-start.5
  257.4 1.3 copy-start.1
Sparse Core Ops, SparseCore 0:
  10.1 68.0 all-gather.1
  84.1 112.5 reduce-scatter.2
  202.7 445.8 all-reduce.1
  651.8 146.2 reduce-scatter.4
where the time goes:
time: 806 us
  waiting for transfers between devices  722 us (90%)
  blocking collectives  52.1 us (6%)
  between operations  13.9 us (2%)
  local copies, waits for them, and re-layouts  8.49 us (1%)
    psum x1, waiting for transfers between devices, per_device(): grad_weight = lax.psum(weight_part, ('row', 'col'))  390 us
    reduce_scatter x1, waiting for transfers between devices, per_device(): lax.psum_scatter(partial_cols.reshape(-1, width), 'row', scatter_dimensio...  150 us
    reduce_scatter x1, waiting for transfers between devices, per_device(): lax.psum_scatter(partial_rows.reshape(-1, width), 'col', scatter_dimensio...  113 us
    all_gather x1, waiting for transfers between devices, per_device(): col_block = lax.all_gather(features, 'row', axis=0, tiled=True)  69.6 us
    all_gather x1, blocking collectives, per_device(): row_block = lax.all_gather(dzed, 'col', axis=0, tiled=True)  52.1 us
  transfers between devices with their start and end apart: 4, of which 4 were waited for; matrix products, arithmetic and copies ran while one was open for 1% of the time, Pallas kernels for 0%

commit v1 on v0

--- a/solution.py
+++ b/solution.py
@@ -13,7 +13,10 @@
     width = features.shape[1]
     n_row = lax.axis_size("row")
     n_col = lax.axis_size("col")
-    col_block = lax.all_gather(features, "row", axis=0, tiled=True)
+    peers = lax.axis_size("row")
+    pieces = jnp.stack([features for _ in range(peers)])
+    pieces = lax.all_to_all(pieces, "row", split_axis=0, concat_axis=0)
+    col_block = jnp.concatenate(pieces, axis=0)
     picked = col_block.reshape(-1, tile, width)[cols_id]
     prods = jnp.einsum("tab,tbf->taf", blocks, picked, preferred_element_type=jnp.float32)
     partial_rows = jax.ops.segment_sum(prods, rows_id, num_segments=n_col * owned // tile)

time: 806 us -> 775 us (0.962)
  the two profiles are of different devices: /device:TPU:16 before, /device:TPU:8 now
where the time goes in v1:
time: 775 us; the launch traced here: 774 us
  waiting for transfers between devices  680 us (88%)
  blocking collectives  53.8 us (7%)
  between operations  13.9 us (2%)
  local copies, waits for them, and re-layouts  9.25 us (1%)
  starting transfers between devices  8.87 us (1%)
    psum x1, waiting for transfers between devices, per_device(): grad_weight = lax.psum(weight_part, ('row', 'col'))  388 us
    reduce_scatter x1, waiting for transfers between devices, per_device(): lax.psum_scatter(partial_cols.reshape(-1, width), 'row', scatter_dimensio...  149 us
    reduce_scatter x1, waiting for transfers between devices, per_device(): lax.psum_scatter(partial_rows.reshape(-1, width), 'col', scatter_dimensio...  114 us
    all_gather x1, blocking collectives, per_device(): row_block = lax.all_gather(dzed, 'col', axis=0, tiled=True)  53.8 us
    all_to_all x1, waiting for transfers between devices, per_device(): pieces = lax.all_to_all(pieces, 'row', split_axis=0, concat_axis=0)  27.8 us
  transfers between devices with their start and end apart: 4, of which 4 were waited for; matrix products, arithmetic and copies ran while one was open for 1% of the time, Pallas kernels for 0%

profile of v1, /device:TPU:8, one launch (start us, length us, event | category | flops | bytes accessed | tf_op | source)
XLA Modules:
  0.0 774.2 jit_solution(240425382897491113)
XLA Ops:
  7.2 0.0 copy-start
  7.2 2.0 stack.2
  9.2 8.8 %all-to-all-start = ((bf16[32,128,128]{2,1,0:T(8,128)(2,1)}), bf16[32,128,128]{2,1,0:T(8,128)(2,1)S(1)}, u32[]{:S(2)}, u32[]{:S(2)}) async-start(bf16[32,128,128]{2,1,0:T(8,128)(2,1)} %stack.2), calls=%async_computation | async-start | bytes 2097152 | tf_op jit(solution)/shard_map/all_to_all | solution.py:18
  18.0 0.0 reduce-scatter.3.cloned.1.call-start
  18.0 0.0 copy-done.5
  18.1 27.8 %all-to-all-done = bf16[32,128,128]{2,1,0:T(8,128)(2,1)S(1)} async-done(((bf16[32,128,128]{2,1,0:T(8,128)(2,1)}), bf16[32,128,128]{2,1,0:T(8,128)(2,1)S(1)}, u32[]{:S(2)}, u32[]{:S(2)}) %all-to-all-start) | async-done | bytes 1048608 | tf_op jit(solution)/shard_map/all_to_all | solution.py:18
  45.8 0.6 gather_fusion
  46.5 0.5 convolution_bitcast_fusion.1
  47.0 0.3 copy.12
  47.3 0.1 broadcast_in_dim.8
  47.4 0.2 copy-done.4
  47.7 1.6 scatter_fusion
  49.3 1.0 copy-done.2
  50.2 0.0 reduce-scatter.3.cloned.1.call-update
  50.2 0.0 all-reduce.2.cloned.1.call-start
  50.3 114.2 %reduce-scatter.3.cloned.1.call-done = f32[128,128]{1,0:T(8,128)} async-done(((f32[2048,128]{1,0:T(8,128)}), f32[128,128]{1,0:T(8,128)}) %reduce-scatter.3.cloned.1.call-update) | async-done | bytes 65552 | tf_op jit(solution)/shard_map/reduce_scatter | solution.py:23
  164.5 1.6 multiply_convert_fusion
  166.2 0.1 convolution_convert_fusion
  166.3 1.7 fusion.3
  168.0 0.0 all-reduce.2.cloned.1.call-update
  168.0 0.0 reduce-scatter.5.cloned.1.call-start
  168.1 53.8 %all_gather.3 = bf16[2048,128]{1,0:T(8,128)(2,1)S(1)} all-gather(bf16[128,128]{1,0:T(8,128)(2,1)S(1)} %convolution_convert_fusion), channel_id=1, replica_groups=mesh['row'=32,'col'=16] {'col'}, dimensions={0}, use_global_device_ids=true | all-gather | bytes 557056 | tf_op jit(solution)/shard_map/all_gather | solution.py:38
  221.8 0.6 gather_fusion.1
  222.5 0.4 convolution_bitcast_fusion
  222.9 1.3 copy.14
  224.2 0.2 broadcast_in_dim.9
  224.4 2.6 scatter_fusion.1
  227.0 1.3 copy-done.1
  228.3 0.0 reduce-scatter.5.cloned.1.call-update
  228.4 388.4 %all-reduce.2.cloned.1.call-done = f32[128,128]{1,0:T(8,128)} async-done(((f32[128,128]{1,0:T(8,128)}), f32[128,128]{1,0:T(8,128)}) %all-reduce.2.cloned.1.call-update) | async-done | bytes 65552 | tf_op jit(solution)/shard_map/psum | solution.py:34
  616.8 149.4 %reduce-scatter.5.cloned.1.call-done = f32[128,128]{1,0:T(8,128)} async-done(((f32[4096,128]{1,0:T(8,128)}), f32[128,128]{1,0:T(8,128)}) %reduce-scatter.5.cloned.1.call-update) | async-done | bytes 65552 | tf_op jit(solution)/shard_map/reduce_scatter | solution.py:42
  766.2 1.5 copy.20
  (13 shorter events, 0.0 us)
Async XLA Ops:
  7.2 39.3 %copy-start = (bf16[1,1,16,128,128]{4,3,2,1,0:T(8,128)(2,1)S(1)}, bf16[1,1,16,128,128]{4,3,2,1,0:T(8,128)(2,1)}, u32[]{:S(2)}) copy-start(bf16[1,1,16,128,128]{4,3,2,1,0:T(8,128)(2,1)} %param.8) | copy-start | bytes 1572868
  7.2 10.8 %copy-start.5 = (s32[1,1,16]{2,1,0:T(1,128)S(1)}, s32[1,1,16]{2,1,0:T(1,128)}, u32[]{:S(2)}) copy-start(s32[1,1,16]{2,1,0:T(1,128)} %param.10) | copy-start | bytes 196
  9.2 36.6 %all-to-all-start = ((bf16[32,128,128]{2,1,0:T(8,128)(2,1)}), bf16[32,128,128]{2,1,0:T(8,128)(2,1)S(1)}, u32[]{:S(2)}, u32[]{:S(2)}) async-start(bf16[32,128,128]{2,1,0:T(8,128)(2,1)} %stack.2), calls=%async_computation | async-start | bytes 2097152 | tf_op jit(solution)/shard_map/all_to_all | solution.py:18
  18.0 146.6 %reduce-scatter.3.cloned.1.call-start = ((), (), s32[]{:S(2)}) async-start(), calls=%async_computation.3 | async-start | bytes 1114112 | tf_op jit(solution)/shard_map/reduce_scatter | solution.py:23
  47.0 0.7 copy-start.4
  47.6 116.9 %copy-start.3 = (bf16[128,128]{1,0:T(8,128)(2,1)S(1)}, bf16[128,128]{1,0:T(8,128)(2,1)}, u32[]{:S(2)}) copy-start(bf16[128,128]{1,0:T(8,128)(2,1)} %param.7) | copy-start | bytes 98308
  47.6 116.9 %copy-start.6 = (bf16[128,128]{1,0:T(8,128)(2,1)S(1)}, bf16[128,128]{1,0:T(8,128)(2,1)}, u32[]{:S(2)}) copy-start(bf16[128,128]{1,0:T(8,128)(2,1)} %param.11) | copy-start | bytes 98308
  49.3 1.0 copy-start.2
  50.2 566.5 %all-reduce.2.cloned.1.call-start = ((), (), s32[]{:S(2)}) async-start(), calls=%async_computation.5 | async-start | bytes 131072 | tf_op jit(solution)/shard_map/psum | solution.py:34
  168.0 598.2 %reduce-scatter.5.cloned.1.call-start = ((), (), s32[]{:S(2)}) async-start(), calls=%async_computation.4 | async-start | bytes 2162688 | tf_op jit(solution)/shard_map/reduce_scatter | solution.py:42
  227.0 1.3 copy-start.1
Sparse Core Ops, SparseCore 0:
  50.4 114.1 reduce-scatter.2
  170.5 446.1 all-reduce.1
  620.1 145.9 reduce-scatter.4
